TPU v7x, 256 devices: a whole 4x4x8 slice. The times are simulated.
256 devices in a mesh: rows: 8 (over x, core), protos: 32 (over y, z).
Axes of the slice: x: 4, y: 4, z: 8, core: 2. Of those that a mesh axis runs over, the one named last changes fastest.
Arguments:
- teacher_features: bfloat16 [4096, 384], P(('rows', 'protos')), may hold values from -80 to 80, as said below
- student_features: bfloat16 [4096, 384], P(('rows', 'protos')), may hold values from -80 to 80, as said below
- prototypes: bfloat16 [131072, 384], P('protos'), may hold values from -80 to 80, as said below
Outputs:
- feature_grad: float32 [4096, 384], P(('rows', 'protos'))
- proto_grad: float32 [8, 16384, 384], P('rows', 'protos')
Inputs may be any that keep to these rules, and one draw needn't show every extreme that they name: `teacher_features`: every row has nonzero entries. `student_features`: every row has nonzero entries. `prototypes`: every row has nonzero entries.
All inputs are finite; a program needn't handle non-finite values.
Results may differ from a plain program's by a relative error of at most 0.012.
The roundings to bfloat16 on the way count: a program that leaves them out, or rounds other values in their place, can miss the bound.
Values may be sent and summed in bfloat16 or wider, within the bound.
A program may use at most 64 MiB of HBM per device.

v0:
```python
import math
import jax
import jax.numpy as jnp
from jax import lax
from jax.sharding import PartitionSpec as P

D = 384
K = 131072
PASSES = 3
eps = 1e-06


def unitize(values):
    values = values.astype(jnp.float32)
    return (values * lax.rsqrt(jnp.sum(values * values, axis=1, keepdims=True) + eps)).astype(
        jnp.bfloat16
    )


def against(left, right):
    return lax.dot_general(
        left, right, (((1,), (1,)), ((), ())), preferred_element_type=jnp.float32
    )


def on_device(teacher_features, student_features, prototypes):
    scale = 1.5 * math.sqrt(D)
    unit_w = unitize(prototypes)
    local_t = unitize(teacher_features)
    local_s = unitize(student_features)
    unit_t, unit_s = (
        lax.all_gather(local_t, "protos", axis=0, tiled=True),
        lax.all_gather(local_s, "protos", axis=0, tiled=True),
    )
    kernel = jnp.exp(scale * against(unit_t, unit_w))
    powers = jnp.exp(scale * against(unit_s, unit_w))
    student_part = jnp.sum(powers, axis=1)
    student_whole = lax.psum(student_part, "protos")
    row_scale = jnp.ones((kernel.shape[0],), jnp.float32)
    col_scale = jnp.ones((kernel.shape[1],), jnp.float32)
    for step in range(PASSES):
        col_part = jnp.dot(row_scale, kernel, precision=lax.Precision.HIGHEST)
        col_scale = 1.0 / lax.psum(col_part, "rows")
        row_part = jnp.dot(kernel, col_scale, precision=lax.Precision.HIGHEST)
        if step == 0:
            row_whole = lax.psum(row_part, "protos")
        else:
            row_whole = lax.psum(row_part, "protos")
        row_scale = 1.0 / row_whole
    target = kernel * row_scale[:, None] * col_scale[None, :]
    probs = powers / student_whole[:, None]
    delta = (probs - target).astype(jnp.bfloat16)
    feature_term = scale * jnp.dot(delta, unit_w, preferred_element_type=jnp.float32)
    feature_grad = lax.psum_scatter(feature_term, "protos", scatter_dimension=0, tiled=True)
    row_groups = lax.axis_size("rows")
    total_rows = delta.shape[0] * row_groups
    factor = scale * K / total_rows
    block = delta.shape[1] // row_groups
    term = factor * lax.dot_general(
        delta, unit_s, (((0,), (0,)), ((), ())), preferred_element_type=jnp.float32
    )
    proto_grad = lax.psum_scatter(
        term.reshape(row_groups, block, term.shape[1]), "rows", scatter_dimension=0, tiled=True
    )
    return (feature_grad, proto_grad)


def solution(mesh):
    return jax.shard_map(
        on_device,
        mesh=mesh,
        in_specs=(P(("rows", "protos"), None), P(("rows", "protos"), None), P("protos", None)),
        out_specs=(P(("rows", "protos"), None), P("rows", "protos", None)),
        check_vma=False,
    )
```

profile of v0, /device:TPU:1, one launch (start us, length us, event | category | flops | bytes accessed | tf_op | source)
XLA Modules:
  0.0 735.6 jit_solution(5828482277272511359)
XLA Ops:
  7.2 0.0 reduce-scatter.3.cloned.1.call-start
  7.2 0.8 fusion.5
  8.0 0.8 fusion.3
  8.9 0.8 fusion.4
  9.7 0.8 fusion.6
  10.4 2.6 fusion.1
  13.0 0.0 copy-start.3
  13.1 41.6 %all_gather.6 = bf16[512,384]{1,0:T(8,128)(2,1)S(1)} all-gather(bf16[16,384]{1,0:T(8,128)(2,1)S(1)} %fusion.4), channel_id=1, replica_groups=mesh['rows'=8,'protos'=32] {'protos'}, dimensions={0}, use_global_device_ids=true | all-gather | bytes 405504 | tf_op jit(solution)/shard_map/all_gather | solution.py:33
  54.6 36.7 %all_gather.7 = bf16[512,384]{1,0:T(8,128)(2,1)S(1)} all-gather(bf16[16,384]{1,0:T(8,128)(2,1)S(1)} %fusion.6), channel_id=1, replica_groups=mesh['rows'=8,'protos'=32] {'protos'}, dimensions={0}, use_global_device_ids=true | all-gather | bytes 405504 | tf_op jit(solution)/shard_map/all_gather | solution.py:32
  91.3 4.3 multiply_exponential_fusion
  95.7 0.0 copy-start
  95.7 3.2 copy-done
  98.9 4.0 fusion.7
  102.9 0.0 copy-done.3
  102.9 44.7 %psum.50 = f32[4096]{0:T(1024)S(1)} all-reduce(f32[4096]{0:T(1024)S(1)} %bitcast.34), channel_id=1, replica_groups=mesh['rows'=8,'protos'=32] {'rows'}, use_global_device_ids=true, to_apply=%region_5.0 | all-reduce | flops 4096 | bytes 32768 | tf_op jit(solution)/shard_map/psum | solution.py:43
  147.7 9.4 %fusion.14 = f32[1,512]{1,0:T(1,128)S(1)} fusion(f32[512,4096]{1,0:T(8,128)} %copy-done, f32[4096,1]{0,1:T(1,128)S(1)} %bitcast.30), kind=kOutput, calls=%fused_computation.31 | convolution fusion | flops 25165824 | bytes 8407040 | tf_op jit(solution)/shard_map/dot_general | solution.py:44
  157.1 58.6 %psum.51 = f32[512]{0:T(512)S(1)} all-reduce(f32[512]{0:T(512)S(1)} %bitcast.36), channel_id=1, replica_groups=mesh['rows'=8,'protos'=32] {'protos'}, use_global_device_ids=true, to_apply=%region_6.0 | all-reduce | flops 512 | bytes 4096 | tf_op jit(solution)/shard_map/psum | solution.py:46
  215.7 6.3 fusion.15
  222.1 37.4 %psum.52 = f32[4096]{0:T(1024)S(1)} all-reduce(f32[4096]{0:T(1024)S(1)} %bitcast.31), channel_id=1, replica_groups=mesh['rows'=8,'protos'=32] {'rows'}, use_global_device_ids=true, to_apply=%region_7.0 | all-reduce | flops 4096 | bytes 32768 | tf_op jit(solution)/shard_map/psum | solution.py:43
  259.5 9.4 %fusion.16 = f32[1,512]{1,0:T(1,128)S(1)} fusion(f32[512,4096]{1,0:T(8,128)} %copy-done, f32[4096,1]{0,1:T(1,128)S(1)} %bitcast.32), kind=kOutput, calls=%fused_computation.33 | convolution fusion | flops 25165824 | bytes 8407040 | tf_op jit(solution)/shard_map/dot_general | solution.py:44
  268.9 55.8 %psum.53 = f32[512]{0:T(512)S(1)} all-reduce(f32[512]{0:T(512)S(1)} %bitcast.38), channel_id=1, replica_groups=mesh['rows'=8,'protos'=32] {'protos'}, use_global_device_ids=true, to_apply=%region_8.0 | all-reduce | flops 512 | bytes 4096 | tf_op jit(solution)/shard_map/psum | solution.py:48
  324.7 0.0 copy-start.1
  324.7 6.5 fusion.17
  331.2 37.6 %psum.54 = f32[4096]{0:T(1024)} all-reduce(f32[4096]{0:T(1024)S(1)} %bitcast.33), channel_id=1, replica_groups=mesh['rows'=8,'protos'=32] {'rows'}, use_global_device_ids=true, to_apply=%region_9.0 | all-reduce | flops 4096 | bytes 32768 | tf_op jit(solution)/shard_map/psum | solution.py:43
  368.8 0.7 broadcast_divide_fusion
  369.6 10.0 %fusion.18 = f32[1,512]{1,0:T(1,128)} fusion(f32[512,4096]{1,0:T(8,128)} %copy-done, f32[4096,1]{0,1:T(1,128)S(1)} %bitcast.29), kind=kOutput, calls=%fused_computation.35 | convolution fusion | flops 25165824 | bytes 8407040 | tf_op jit(solution)/shard_map/dot_general | solution.py:44
  379.6 0.0 copy-done.1
  379.6 6.2 fusion
  385.8 58.2 %all-reduce = (f32[512]{0:T(512)}, f32[512]{0:T(512)}) all-reduce(f32[512]{0:T(512)} %bitcast.35, f32[512]{0:T(512)} %get-tuple-element.4), channel_id=1, replica_groups=mesh['rows'=8,'protos'=32] {'protos'}, use_global_device_ids=true, to_apply=%region_10.0 | all-reduce | flops 1024 | bytes 8192 | tf_op jit(solution)/shard_map/psum | solution.py:48
  444.0 0.7 broadcast_divide_fusion.5
  444.6 0.0 copy-start.4
  444.6 7.3 subtract_convert_fusion
  452.0 0.0 copy-start.2
  452.0 2.0 copy-done.2
  454.0 0.0 copy-done.4
  454.0 3.3 convolution_multiply_fusion.1
  457.4 0.0 reduce-scatter.3.cloned.1.call-update
  457.4 0.0 reduce-scatter.5.cloned.1.call-start
  457.4 7.2 convolution_multiply_fusion
  464.7 0.0 reduce-scatter.5.cloned.1.call-update
  464.7 212.9 %reduce-scatter.3.cloned.1.call-done = f32[16,384]{1,0:T(8,128)} async-done(((f32[512,384]{1,0:T(8,128)}), f32[16,384]{1,0:T(8,128)}) %reduce-scatter.3.cloned.1.call-update) | async-done | bytes 24592 | tf_op jit(solution)/shard_map/reduce_scatter | solution.py:54
  677.6 51.2 %reduce-scatter.5.cloned.1.call-done = f32[1,512,384]{2,1,0:T(8,128)} async-done(((f32[8,512,384]{2,1,0:T(8,128)}), f32[1,512,384]{2,1,0:T(8,128)}) %reduce-scatter.5.cloned.1.call-update) | async-done | bytes 786448 | tf_op jit(solution)/shard_map/reduce_scatter | solution.py:62
  (7 shorter events, 0.0 us)
Async XLA Ops:
  7.2 670.4 %reduce-scatter.3.cloned.1.call-start = ((), (), s32[]{:S(2)}) async-start(), calls=%async_computation.2 | async-start | bytes 811008 | tf_op jit(solution)/shard_map/reduce_scatter | solution.py:54
  13.0 89.9 %copy-start.3 = (f32[4096]{0:T(1024)}, f32[4096]{0:T(1024)S(1)}, u32[]{:S(2)}) copy-start(f32[4096]{0:T(1024)S(1)} %add_rsqrt_fusion) | copy-start | bytes 49156
  95.7 3.2 copy-start
  324.7 54.9 %copy-start.1 = (bf16[4096,384]{1,0:T(8,128)(2,1)S(1)}, bf16[4096,384]{1,0:T(8,128)(2,1)}, u32[]{:S(2)}) copy-start(bf16[4096,384]{1,0:T(8,128)(2,1)} %param.5) | copy-start | bytes 9437188
  444.6 9.4 %copy-start.4 = (f32[4096]{0:T(1024)S(1)}, f32[4096]{0:T(1024)}, u32[]{:S(2)}) copy-start(f32[4096]{0:T(1024)} %copy-done.3) | copy-start | bytes 49156
  452.0 2.0 copy-start.2
  457.4 271.4 %reduce-scatter.5.cloned.1.call-start = ((), (), s32[]{:S(2)}) async-start(), calls=%async_computation.3 | async-start | bytes 7077888 | tf_op jit(solution)/shard_map/reduce_scatter | solution.py:62
Sparse Core Ops, SparseCore 0:
  457.5 220.0 reduce-scatter.2
  680.7 48.0 reduce-scatter.4
where the time goes:
time: 736 us
  blocking collectives  371 us (50%)
  waiting for transfers between devices  264 us (36%)
  matrix products  66.9 us (9%)
  other arithmetic  14.6 us (2%)
  between operations  14.1 us (2%)
    reduce_scatter x1, waiting for transfers between devices, on_device(): lax.psum_scatter(feature_term, 'protos', scatter_dimension=0, tiled=True)  213 us
    psum x3, blocking collectives, on_device(): row_whole = lax.psum(row_part, 'protos')  173 us
    psum x3, blocking collectives, on_device(): col_scale = 1.0 / lax.psum(col_part, 'rows')  120 us
    reduce_scatter x1, waiting for transfers between devices, on_device(): lax.psum_scatter(term.reshape(row_groups, block, term.shape[1]), 'rows',...  51.2 us
    all_gather x1, blocking collectives, on_device(): lax.all_gather(local_s, 'protos', axis=0, tiled=True)  41.6 us
    all_gather x1, blocking collectives, on_device(): lax.all_gather(local_t, 'protos', axis=0, tiled=True)  36.7 us
    dot_general x3, matrix products, on_device(): row_part = jnp.dot(kernel, col_scale, precision=lax.Precision.HIGHEST)  28.9 us
    dot_general x3, matrix products, on_device(): col_part = jnp.dot(row_scale, kernel, precision=lax.Precision.HIGHEST)  16.9 us
  transfers between devices with their start and end apart: 2, of which 2 were waited for; matrix products, arithmetic and copies ran while one was open for 1% of the time, Pallas kernels for 0%

commit v1 on v0

--- a/solution.py
+++ b/solution.py
@@ -43,7 +43,7 @@
         col_scale = 1.0 / lax.psum(col_part, "rows")
         row_part = jnp.dot(kernel, col_scale, precision=lax.Precision.HIGHEST)
         if step == 0:
-            row_whole = lax.psum(row_part, "protos")
+            row_whole = jnp.sum(lax.all_gather(row_part, "protos"), axis=0)
         else:
             row_whole = lax.psum(row_part, "protos")
         row_scale = 1.0 / row_whole

time: 736 us -> 713 us (0.969)
  blocking collectives: 371 us -> 346 us
    psum x3 -> x2, blocking collectives: 173 us -> 115 us  [on_device(): row_whole = lax.psum(row_part, 'protos')]
    all_gather x0 -> x1, blocking collectives: none -> 34.7 us  [on_device(): row_whole = jnp.sum(lax.all_gather(row_part, 'protos'), axis=0)]
where the time goes in v1:
time: 713 us
  blocking collectives  346 us (49%)
  waiting for transfers between devices  266 us (37%)
  matrix products  66.8 us (9%)
  other arithmetic  14.7 us (2%)
  between operations  14.1 us (2%)
    reduce_scatter x1, waiting for transfers between devices, on_device(): lax.psum_scatter(feature_term, 'protos', scatter_dimension=0, tiled=True)  215 us
    psum x3, blocking collectives, on_device(): col_scale = 1.0 / lax.psum(col_part, 'rows')  118 us
    psum x2, blocking collectives, on_device(): row_whole = lax.psum(row_part, 'protos')  115 us
    reduce_scatter x1, waiting for transfers between devices, on_device(): lax.psum_scatter(term.reshape(row_groups, block, term.shape[1]), 'rows',...  51.2 us
    all_gather x1, blocking collectives, on_device(): lax.all_gather(local_s, 'protos', axis=0, tiled=True)  41.6 us
    all_gather x1, blocking collectives, on_device(): lax.all_gather(local_t, 'protos', axis=0, tiled=True)  36.7 us
    all_gather x1, blocking collectives, on_device(): row_whole = jnp.sum(lax.all_gather(row_part, 'protos'), axis=0)  34.7 us
    dot_general x3, matrix products, on_device(): row_part = jnp.dot(kernel, col_scale, precision=lax.Precision.HIGHEST)  28.9 us
  transfers between devices with their start and end apart: 2, of which 2 were waited for; matrix products, arithmetic and copies ran while one was open for 1% of the time, Pallas kernels for 0%

profile of v1, /device:TPU:1, one launch (start us, length us, event | category | flops | bytes accessed | tf_op | source)
XLA Modules:
  0.0 712.6 jit_solution(18410232759558618920)
XLA Ops:
  7.2 0.0 reduce-scatter.3.cloned.1.call-start
  7.2 0.8 fusion.5
  8.0 0.8 fusion.3
  8.9 0.8 fusion.4
  9.7 0.8 fusion.6
  10.4 2.6 fusion.1
  13.0 0.0 copy-start.3
  13.1 41.6 %all_gather.12 = bf16[512,384]{1,0:T(8,128)(2,1)S(1)} all-gather(bf16[16,384]{1,0:T(8,128)(2,1)S(1)} %fusion.4), channel_id=1, replica_groups=mesh['rows'=8,'protos'=32] {'protos'}, dimensions={0}, use_global_device_ids=true | all-gather | bytes 405504 | tf_op jit(solution)/shard_map/all_gather | solution.py:33
  54.6 36.7 %all_gather.13 = bf16[512,384]{1,0:T(8,128)(2,1)S(1)} all-gather(bf16[16,384]{1,0:T(8,128)(2,1)S(1)} %fusion.6), channel_id=1, replica_groups=mesh['rows'=8,'protos'=32] {'protos'}, dimensions={0}, use_global_device_ids=true | all-gather | bytes 405504 | tf_op jit(solution)/shard_map/all_gather | solution.py:32
  91.3 4.3 multiply_exponential_fusion
  95.7 0.0 copy-start
  95.7 3.2 copy-done
  98.9 4.0 fusion.7
  102.9 0.0 copy-done.3
  102.9 44.7 %psum.43 = f32[4096]{0:T(1024)S(1)} all-reduce(f32[4096]{0:T(1024)S(1)} %bitcast.37), channel_id=1, replica_groups=mesh['rows'=8,'protos'=32] {'rows'}, use_global_device_ids=true, to_apply=%region_5.0 | all-reduce | flops 4096 | bytes 32768 | tf_op jit(solution)/shard_map/psum | solution.py:43
  147.7 9.4 %convolution_bitcast_fusion = f32[1,1,512]{2,1,0:T(1,128)S(1)} fusion(f32[512,4096]{1,0:T(8,128)} %copy-done, f32[4096,1]{0,1:T(1,128)S(1)} %bitcast.33), kind=kOutput, calls=%fused_computation.10 | convolution fusion | flops 25165824 | bytes 8407040 | tf_op jit(solution)/shard_map/dot_general | solution.py:44
  157.1 34.7 %all-gather.1 = f32[32,1,512]{2,1,0:T(1,128)S(1)} all-gather(f32[1,1,512]{2,1,0:T(1,128)S(1)} %convolution_bitcast_fusion), channel_id=2, replica_groups=mesh['rows'=8,'protos'=32] {'protos'}, dimensions={0}, use_global_device_ids=true | all-gather | bytes 67584 | tf_op jit(solution)/shard_map/all_gather | solution.py:46
  191.8 0.1 reduce_sum.49
  191.9 6.3 fusion.14
  198.3 35.7 %psum.44 = f32[4096]{0:T(1024)S(1)} all-reduce(f32[4096]{0:T(1024)S(1)} %bitcast.34), channel_id=1, replica_groups=mesh['rows'=8,'protos'=32] {'rows'}, use_global_device_ids=true, to_apply=%region_7.0 | all-reduce | flops 4096 | bytes 32768 | tf_op jit(solution)/shard_map/psum | solution.py:43
  233.9 9.4 %fusion.15 = f32[1,512]{1,0:T(1,128)S(1)} fusion(f32[512,4096]{1,0:T(8,128)} %copy-done, f32[4096,1]{0,1:T(1,128)S(1)} %bitcast.35), kind=kOutput, calls=%fused_computation.33 | convolution fusion | flops 25165824 | bytes 8407040 | tf_op jit(solution)/shard_map/dot_general | solution.py:44
  243.4 58.4 %psum.45 = f32[512]{0:T(512)S(1)} all-reduce(f32[512]{0:T(512)S(1)} %bitcast.40), channel_id=1, replica_groups=mesh['rows'=8,'protos'=32] {'protos'}, use_global_device_ids=true, to_apply=%region_8.0 | all-reduce | flops 512 | bytes 4096 | tf_op jit(solution)/shard_map/psum | solution.py:48
  301.8 0.0 copy-start.1
  301.8 6.5 fusion.16
  308.3 37.6 %psum.46 = f32[4096]{0:T(1024)} all-reduce(f32[4096]{0:T(1024)S(1)} %bitcast.36), channel_id=1, replica_groups=mesh['rows'=8,'protos'=32] {'rows'}, use_global_device_ids=true, to_apply=%region_9.0 | all-reduce | flops 4096 | bytes 32768 | tf_op jit(solution)/shard_map/psum | solution.py:43
  345.9 0.7 broadcast_divide_fusion
  346.7 10.0 %fusion.17 = f32[1,512]{1,0:T(1,128)} fusion(f32[512,4096]{1,0:T(8,128)} %copy-done, f32[4096,1]{0,1:T(1,128)S(1)} %bitcast.32), kind=kOutput, calls=%fused_computation.35 | convolution fusion | flops 25165824 | bytes 8407040 | tf_op jit(solution)/shard_map/dot_general | solution.py:44
  356.7 0.0 copy-done.1
  356.7 6.2 fusion
  362.9 56.4 %all-reduce = (f32[512]{0:T(512)}, f32[512]{0:T(512)}) all-reduce(f32[512]{0:T(512)} %bitcast.38, f32[512]{0:T(512)} %get-tuple-element.4), channel_id=1, replica_groups=mesh['rows'=8,'protos'=32] {'protos'}, use_global_device_ids=true, to_apply=%region_10.0 | all-reduce | flops 1024 | bytes 8192 | tf_op jit(solution)/shard_map/psum | solution.py:48
  419.3 0.7 broadcast_divide_fusion.5
  420.0 0.0 copy-start.4
  420.0 7.3 %subtract_convert_fusion = bf16[512,4096]{1,0:T(8,128)(2,1)S(1)} fusion(f32[512,4096]{1,0:T(8,128)} %copy-done, f32[512,4096]{1,0:T(8,128)} %get-tuple-element.5, f32[4096]{0:T(1024)S(1)} %broadcast_divide_fusion, f32[512]{0:T(512)S(1)} %broadcast_divide_fusion.5, f32[512]{0:T(512)} %get-tuple-element.3), kind=kLoop, calls=%fused_computation | loop fusion | flops 12582912 | bytes 20992000 | tf_op jit(solution)/shard_map/convert_element_type | solution.py:52
  427.3 0.0 copy-start.2
  427.3 2.0 copy-done.2
  429.4 0.0 copy-done.4
  429.4 3.3 convolution_multiply_fusion.1
  432.7 0.0 reduce-scatter.3.cloned.1.call-update
  432.7 0.0 reduce-scatter.5.cloned.1.call-start
  432.8 7.2 %convolution_multiply_fusion = f32[4096,384]{1,0:T(8,128)} fusion(bf16[512,4096]{1,0:T(8,128)(2,1)} %copy-done.2, bf16[512,384]{1,0:T(8,128)(2,1)S(1)} %all_gather.12), kind=kOutput, calls=%fused_computation.8 | convolution fusion | flops 1612185600 | bytes 10878976 | tf_op jit(solution)/shard_map/dot_general | solution.py:59
  440.0 0.0 reduce-scatter.5.cloned.1.call-update
  440.0 214.5 %reduce-scatter.3.cloned.1.call-done = f32[16,384]{1,0:T(8,128)} async-done(((f32[512,384]{1,0:T(8,128)}), f32[16,384]{1,0:T(8,128)}) %reduce-scatter.3.cloned.1.call-update) | async-done | bytes 24592 | tf_op jit(solution)/shard_map/reduce_scatter | solution.py:54
  654.6 51.2 %reduce-scatter.5.cloned.1.call-done = f32[1,512,384]{2,1,0:T(8,128)} async-done(((f32[8,512,384]{2,1,0:T(8,128)}), f32[1,512,384]{2,1,0:T(8,128)}) %reduce-scatter.5.cloned.1.call-update) | async-done | bytes 786448 | tf_op jit(solution)/shard_map/reduce_scatter | solution.py:62
  (7 shorter events, 0.0 us)
Async XLA Ops:
  7.2 647.4 %reduce-scatter.3.cloned.1.call-start = ((), (), s32[]{:S(2)}) async-start(), calls=%async_computation.2 | async-start | bytes 811008 | tf_op jit(solution)/shard_map/reduce_scatter | solution.py:54
  13.0 89.9 %copy-start.3 = (f32[4096]{0:T(1024)}, f32[4096]{0:T(1024)S(1)}, u32[]{:S(2)}) copy-start(f32[4096]{0:T(1024)S(1)} %add_rsqrt_fusion) | copy-start | bytes 49156
  95.7 3.2 copy-start
  301.8 54.9 %copy-start.1 = (bf16[4096,384]{1,0:T(8,128)(2,1)S(1)}, bf16[4096,384]{1,0:T(8,128)(2,1)}, u32[]{:S(2)}) copy-start(bf16[4096,384]{1,0:T(8,128)(2,1)} %param.5) | copy-start | bytes 9437188
  420.0 9.4 %copy-start.4 = (f32[4096]{0:T(1024)S(1)}, f32[4096]{0:T(1024)}, u32[]{:S(2)}) copy-start(f32[4096]{0:T(1024)} %copy-done.3) | copy-start | bytes 49156
  427.3 2.0 copy-start.2
  432.7 273.0 %reduce-scatter.5.cloned.1.call-start = ((), (), s32[]{:S(2)}) async-start(), calls=%async_computation.3 | async-start | bytes 7077888 | tf_op jit(solution)/shard_map/reduce_scatter | solution.py:62
Sparse Core Ops, SparseCore 0:
  432.8 221.6 reduce-scatter.2
  657.7 48.0 reduce-scatter.4
